TPU v7x, 256 devices: a whole 4x4x8 slice. The times are simulated.
256 devices in a mesh: tm: 4 (over y), lag: 64 (over x, z, core).
Axes of the slice: x: 4, y: 4, z: 8, core: 2. Of those that a mesh axis runs over, the one named last changes fastest.
Arguments:
- samples: bfloat16 [8192, 512], P(('tm', 'lag')), may hold values from -6 to 6
Outputs:
- upper_gen: float32 [128, 512, 512], P('lag', None, 'tm')
- lower_gen: float32 [128, 512, 512], P('lag', None, 'tm')
All inputs are finite; a program needn't handle non-finite values.
Results may differ from a plain program's by a relative error of at most 0.0003.
Values may be sent and summed in bfloat16 or wider, within the bound.
No kernel may reach another device: no remote copies, remote signals or barrier semaphores. Data moves between devices by JAX's collectives and lax.ppermute only.
A program may use at most 64 MiB of HBM per device.

v0:
```python
import jax
import jax.numpy as jnp
from jax import lax
from jax.sharding import PartitionSpec as P

C = 512
LAG_DEV = 2
TIME = 8192
SCHUR_STEPS = 3


HIGH = lax.Precision.HIGHEST


def passed_along(block, axis, distance):
    devices = range(lax.axis_size(axis))
    route = [(i - distance, i) for i in devices if i - distance in devices]
    return lax.ppermute(block, axis, route)


def spread(value, axis, source):
    kept = jnp.where(lax.axis_index(axis) == source, value, 0).astype(value.dtype)
    return lax.psum(kept, axis)


def solve_coefficient(head, lower_head):
    normal = jnp.dot(head.T, head, precision=HIGH, preferred_element_type=jnp.float32)
    factor = jnp.linalg.cholesky(normal)
    middle = lax.linalg.triangular_solve(factor, head.T, left_side=True, lower=True)
    inverse = lax.linalg.triangular_solve(
        factor, middle, left_side=True, lower=True, transpose_a=True
    )
    return jnp.dot(lower_head, inverse, precision=HIGH, preferred_element_type=jnp.float32)


def shards(samples):
    lag_count = lax.axis_size("lag")
    tm_count = lax.axis_size("tm")
    window = lax.all_gather(samples, "lag", axis=0, tiled=True)
    rows = window.shape[0]
    total_lags = LAG_DEV * lag_count
    tail_rows = passed_along(window[:total_lags], "tm", -1)
    extended = jnp.concatenate([window, tail_rows], axis=0)
    first_lag = lax.axis_index("lag") * LAG_DEV
    partial_value = jnp.stack(
        [
            lax.dot_general(
                lax.dynamic_slice_in_dim(extended, first_lag + offset, rows, 0),
                window,
                (((0,), (0,)), ((), ())),
                preferred_element_type=jnp.float32,
            )
            for offset in range(LAG_DEV)
        ]
    )
    blocks = lax.psum(partial_value, "tm") / jnp.float32(TIME)
    lag_ids = first_lag + jnp.arange(LAG_DEV, dtype=jnp.int32)
    width = C
    share = width // tm_count
    column = lax.axis_index("tm") * share
    upper = blocks
    lower = jnp.where((lag_ids == 0)[:, None, None], jnp.zeros_like(blocks), blocks)
    for schur_step in range(1, SCHUR_STEPS + 1):
        incoming = passed_along(upper[LAG_DEV - 1], "lag", 1)
        upper = jnp.concatenate([incoming[None], upper[: LAG_DEV - 1]], axis=0)
        owner = schur_step // LAG_DEV
        place = schur_step % LAG_DEV
        head = upper[place]
        lower_head = lower[place]
        head, lower_head = (spread(head, "lag", owner), spread(lower_head, "lag", owner))
        coeff = solve_coefficient(head, lower_head)
        new_upper = upper - jnp.einsum("ab,kac->kbc", coeff, lower, precision=HIGH)
        lower = lower - jnp.einsum("ab,kbc->kac", coeff, upper, precision=HIGH)
        upper = new_upper
    upper = lax.dynamic_slice_in_dim(upper, column, share, 2)
    lower = lax.dynamic_slice_in_dim(lower, column, share, 2)
    return (upper, lower)


def solution(mesh):
    placed = (P(("tm", "lag"), None),)
    return jax.shard_map(
        shards,
        mesh=mesh,
        in_specs=placed,
        out_specs=(P("lag", None, "tm"), P("lag", None, "tm")),
        check_vma=False,
    )
```

profile of v0, /device:TPU:8, one launch (start us, length us, event | category | flops | bytes accessed | tf_op | source)
XLA Modules:
  0.0 1275.0 jit_solution(10305898371644061302)
XLA Ops:
  7.9 83.1 %all-gather.2.cloned.1.call-done = bf16[2048,512]{1,0:T(8,128)(2,1)} async-done(((bf16[32,512]{1,0:T(8,128)(2,1)}), bf16[2048,512]{1,0:T(8,128)(2,1)}) %all-gather.2.cloned.1.call-update) | async-done | bytes 2097168 | tf_op jit(solution)/shard_map/all_gather | solution.py:39
  92.0 2.6 collective-permute-start
  96.3 3.3 collective-permute-done
  103.8 60.3 %all-reduce.9.cloned.1.call-done = f32[2,512,512]{2,1,0:T(8,128)} async-done(((f32[2,512,512]{2,1,0:T(8,128)}), f32[2,512,512]{2,1,0:T(8,128)}) %all-reduce.9.cloned.1.call-update) | async-done | bytes 2097168 | tf_op jit(solution)/shard_map/psum | solution.py:56
  169.3 2.7 collective-permute-start.1
  172.0 188.7 %all-reduce.15.cloned.1.call-done = (f32[512,512]{1,0:T(8,128)}, f32[512,512]{1,0:T(8,128)}) async-done(((f32[512,512]{1,0:T(8,128)}, f32[512,512]{1,0:T(8,128)}), (f32[512,512]{1,0:T(8,128)}, f32[512,512]{1,0:T(8,128)})) %all-reduce.15.cloned.1.call-update) | async-done | bytes 2097168 | tf_op jit(solution)/shard_map/psum | solution.py:23
  360.7 3.4 fusion.195
  367.9 11.7 cholesky.374
  379.8 9.8 custom-call.36
  392.1 12.1 cholesky.393
  405.6 9.8 custom-call.37
  418.0 11.7 cholesky.414
  431.0 9.8 custom-call.38
  443.1 11.9 cholesky.431
  458.8 2.4 select_select_fusion.2
  461.2 11.3 while.12
  473.2 40.1 %custom-call.40 = f32[4,128,128]{1,2,0:T(8,128)S(1)} custom-call(f32[4,128,128]{2,1,0:T(8,128)} %copy-done.22), custom_call_target="InvertDiagBlocksLowerTriangular" | custom-call | tf_op jit(solution)/shard_map/triangular_solve/custom-call.8 | solution.py:30
  524.0 5.6 bitcast_subtract_fusion.3
  532.5 5.4 bitcast_subtract_fusion.2
  541.6 197.5 %all-reduce.13.cloned.1.call-done = (f32[512,512]{1,0:T(8,128)}, f32[512,512]{1,0:T(8,128)}) async-done(((f32[512,512]{1,0:T(8,128)}, f32[512,512]{1,0:T(8,128)}), (f32[512,512]{1,0:T(8,128)}, f32[512,512]{1,0:T(8,128)})) %all-reduce.13.cloned.1.call-update) | async-done | bytes 2097168 | tf_op jit(solution)/shard_map/psum | solution.py:23
  739.0 3.4 fusion.196
  744.0 11.7 cholesky.446
  755.9 9.8 custom-call.41
  768.2 11.9 cholesky.465
  781.5 9.8 custom-call.42
  792.9 11.7 cholesky.486
  805.3 9.8 custom-call.43
  816.6 12.1 cholesky.503
  833.0 11.3 while.13
  844.3 39.3 %custom-call.45 = f32[4,128,128]{1,2,0:T(8,128)S(1)} custom-call(f32[4,128,128]{2,1,0:T(8,128)S(1)} %get-tuple-element.48), custom_call_target="InvertDiagBlocksLowerTriangular" | custom-call | tf_op jit(solution)/shard_map/triangular_solve/custom-call.8 | solution.py:30
  894.3 3.6 bitcast_subtract_fusion
  897.9 3.8 bitcast_subtract_fusion.1
  904.8 2.3 collective-permute-start.3
  907.1 187.0 %all-reduce.11.cloned.1.call-done = (f32[512,512]{1,0:T(8,128)}, f32[512,512]{1,0:T(8,128)}) async-done(((f32[512,512]{1,0:T(8,128)}, f32[512,512]{1,0:T(8,128)}), (f32[512,512]{1,0:T(8,128)}, f32[512,512]{1,0:T(8,128)})) %all-reduce.11.cloned.1.call-update) | async-done | bytes 2097168 | tf_op jit(solution)/shard_map/psum | solution.py:23
  1094.1 3.4 fusion.197
  1101.3 11.7 cholesky.518
  1113.2 9.8 custom-call.46
  1125.5 12.1 cholesky.537
  1139.0 9.8 custom-call.47
  1151.4 11.7 cholesky.558
  1164.4 9.8 custom-call.48
  1176.5 11.9 cholesky.575
  1192.2 2.4 select_select_fusion
  1194.6 11.3 while.14
  1195.2 2.2 bitcast_dynamic-update-slice_fusion.8
  1206.6 40.1 %custom-call.50 = f32[4,128,128]{1,2,0:T(8,128)S(1)} custom-call(f32[4,128,128]{2,1,0:T(8,128)} %copy-done.21), custom_call_target="InvertDiagBlocksLowerTriangular" | custom-call | tf_op jit(solution)/shard_map/triangular_solve/custom-call.8 | solution.py:30
  1257.4 3.8 convolution_bitcast_fusion
  1261.2 4.8 fusion.7
  (222 shorter events, 130.3 us)
Async XLA Ops:
  7.2 83.9 %all-gather.2.cloned.1.call-start = ((), (), s32[]{:S(2)}) async-start(), calls=%async_computation | async-start | bytes 2129920 | tf_op jit(solution)/shard_map/all_gather | solution.py:39
  7.9 156.2 %all-reduce.9.cloned.1.call-start = ((), (), s32[]{:S(2)}) async-start(), calls=%async_computation.1 | async-start | bytes 4194304 | tf_op jit(solution)/shard_map/psum | solution.py:56
  91.9 7.7 copy-start.17
  92.0 7.6 collective-permute-start
  103.7 256.9 %all-reduce.15.cloned.1.call-start = ((), (), s32[]{:S(2)}) async-start(), calls=%async_computation.4 | async-start | bytes 4194304 | tf_op jit(solution)/shard_map/psum | solution.py:23
  169.2 569.8 %all-reduce.13.cloned.1.call-start = ((), (), s32[]{:S(2)}) async-start(), calls=%async_computation.3 | async-start | bytes 4194304 | tf_op jit(solution)/shard_map/psum | solution.py:23
  169.3 354.7 %collective-permute-start.1 = (f32[512,512]{1,0:T(8,128)}, f32[512,512]{1,0:T(8,128)}, u32[]{:S(2)}, u32[]{:S(2)}) collective-permute-start(f32[512,512]{1,0:T(8,128)} %get-tuple-element.94), channel_id=1, source_target_pairs={{0,1},{1,2},{2,3},{3,4},{4,5},{5,6},{6,7},{7,8},{8,9},{9,10},{10,1... | collective-permute-start | bytes 3145736 | tf_op jit(solution)/shard_map/ppermute | solution.py:18
  366.9 1.0 copy-start.14
  415.7 1.0 copy-start.9
  418.0 95.4 %copy-start.7 = (f32[512,512]{1,0:T(8,128)S(1)}, f32[512,512]{1,0:T(8,128)}, u32[]{:S(2)}) copy-start(f32[512,512]{1,0:T(8,128)} %get-tuple-element.80) | copy-start | bytes 3145732
  472.5 0.7 copy-start.22
  513.4 2.3 copy-start.13
  519.8 2.3 copy-start.19
  521.7 2.3 copy-start.4
  524.0 5.7 copy-start.2
  531.2 9.2 collective-permute-start.2
  537.9 1.4 copy-start
  541.5 552.6 %all-reduce.11.cloned.1.call-start = ((), (), s32[]{:S(2)}) async-start(), calls=%async_computation.2 | async-start | bytes 4194304 | tf_op jit(solution)/shard_map/psum | solution.py:23
  743.0 1.0 copy-start.15
  792.8 90.8 %copy-start.8 = (f32[512,512]{1,0:T(8,128)S(1)}, f32[512,512]{1,0:T(8,128)}, u32[]{:S(2)}) copy-start(f32[512,512]{1,0:T(8,128)} %get-tuple-element.78) | copy-start | bytes 3145732
  883.7 2.3 copy-start.11
  890.1 2.3 copy-start.20
  892.0 2.3 copy-start.1
  892.0 2.3 copy-start.5
  904.8 356.4 %collective-permute-start.3 = (f32[512,512]{1,0:T(8,128)}, f32[512,512]{1,0:T(8,128)}, u32[]{:S(2)}, u32[]{:S(2)}) collective-permute-start(f32[512,512]{1,0:T(8,128)} %get-tuple-element.89), channel_id=1, source_target_pairs={{0,1},{1,2},{2,3},{3,4},{4,5},{5,6},{6,7},{7,8},{8,9},{9,10},{10,1... | collective-permute-start | bytes 3145736 | tf_op jit(solution)/shard_map/ppermute | solution.py:18
  1100.3 1.0 copy-start.16
  1149.1 1.0 copy-start.10
  1151.4 95.4 %copy-start.6 = (f32[512,512]{1,0:T(8,128)S(1)}, f32[512,512]{1,0:T(8,128)}, u32[]{:S(2)}) copy-start(f32[512,512]{1,0:T(8,128)} %get-tuple-element.76) | copy-start | bytes 3145732
  1205.9 0.7 copy-start.21
  1246.7 2.3 copy-start.12
  1253.2 2.3 copy-start.18
  1257.4 3.9 copy-start.3
Sparse Core Ops, SparseCore 0:
  10.7 80.2 all-gather.1
  103.8 60.2 all-reduce.8
  169.3 191.3 all-reduce.14
  541.6 197.3 all-reduce.12
  904.9 189.1 all-reduce.10
where the time goes:
time: 1280 us; the launch traced here: 1270 us
  waiting for transfers between devices  721 us (56%)
  other arithmetic  384 us (30%)
  matrix products  89.1 us (7%)
  local copies, waits for them, and re-layouts  49.2 us (4%)
  between operations  22.7 us (2%)
    psum x3, waiting for transfers between devices, spread(): return lax.psum(kept, axis)  573 us
    another operation x45, other arithmetic, solve_coefficient(): factor = jnp.linalg.cholesky(normal)  241 us
    another operation x7, other arithmetic, solve_coefficient(): lax.linalg.triangular_solve(factor, middle, left_side=True, lower=True, t...  125 us
    all_gather x1, waiting for transfers between devices, shards(): window = lax.all_gather(samples, 'lag', axis=0, tiled=True)  83.1 us
    psum x1, waiting for transfers between devices, shards(): blocks = lax.psum(partial_value, 'tm') / jnp.float32(TIME)  60.3 us
    another operation x40, local copies, waits for them, and re-layouts, solve_coefficient(): lax.linalg.triangular_solve(factor, middle, left_side=True, lower=True, t...  33.7 us
  transfers between devices with their start and end apart: 9, of which 6 were waited for; matrix products, arithmetic and copies ran while one was open for 26% of the time, Pallas kernels for 0%

commit v1 on v0

v1 whole, which is shorter than its diff:
```python
import functools

import jax
import jax.numpy as jnp
from jax import lax
from jax.experimental import pallas as pl
from jax.experimental.pallas import tpu as pltpu
from jax.sharding import Mesh, PartitionSpec as P

C = 512
LAG_DEV = 2
TIME = 8192
SCHUR_STEPS = 3
BLOCK = 512
HALF = 256
PIECES = (
    (0, (0, -1, 1, 2)),
    (-1, (0, -1, 1, 2)),
    (1, (0, -1, 1, 2)),
    (2, (0, -1)),
    (2, (1, 2)),
)
CHUNK = 2048
PAD = 128
SHARE = 128
LOCAL = LAG_DEV + SCHUR_STEPS
ACCEPT = 1e-4

F32, BF16 = jnp.float32, jnp.bfloat16
HIGHEST = lax.Precision.HIGHEST


def mm(a, b):
    return jnp.dot(a, b, preferred_element_type=F32)


def mm_nt(a, b):
    return lax.dot_general(a, b, (((1,), (1,)), ((), ())), preferred_element_type=F32)


def halves(value):
    high = value.astype(BF16)
    return high, (value - high.astype(F32)).astype(BF16)


def mm3(a, b):
    return mm(a[0], b[0]) + mm(a[0], b[1]) + mm(a[1], b[0])


def eye():
    rows = lax.broadcasted_iota(jnp.int32, (C, C), 0)
    cols = lax.broadcasted_iota(jnp.int32, (C, C), 1)
    return jnp.where(rows == cols, 1.0, 0.0).astype(F32)


def load_blocks(place, sources, xt, sem):
    y, x, core = place[0], place[2], place[3]
    copies = []
    for whose in range(2):
        colour = lax.rem(core + whose, 2)
        for source, (far, nears) in zip(sources[whose], PIECES, strict=True):
            for i, near in enumerate(nears):
                along_x = lax.rem(x + jnp.where(colour == 0, near, far) + 4, 4)
                along_y = lax.rem(y + jnp.where(colour == 0, far, near) + 4, 4)
                start = PAD + (along_y * 4 + along_x) * BLOCK + colour * HALF
                to = xt.at[:, pl.ds(pl.multiple_of(start, HALF // 2), HALF)]
                copies.append(
                    pltpu.make_async_copy(source.at[i], to, sem.at[len(copies)])
                )
    return copies


def products(place, xt, moved, columns, heads, local):
    lag0 = LAG_DEV * place[1] - SCHUR_STEPS
    first = pl.multiple_of(place[0] * SHARE, SHARE)
    wide = CHUNK + PAD
    heads[...] = jnp.zeros_like(heads)
    local[...] = jnp.zeros_like(local)

    def chunk_step(c, carry):
        start = pl.multiple_of(c * CHUNK, CHUNK)
        for shift in range(1, SCHUR_STEPS + 1):
            for row in range(0, C, 128):
                ext = xt[row : row + 128, pl.ds(start + PAD, wide)].astype(F32)
                rolled = pltpu.roll(ext, wide - shift, 1)
                moved[shift - 1, row : row + 128, :] = rolled[:, :CHUNK].astype(BF16)
        for j in range(LOCAL):
            ext = xt[pl.ds(first, SHARE), pl.ds(start, wide)].astype(F32)
            rolled = pltpu.roll(ext, CHUNK + lag0 + j, 1)
            columns[j * SHARE : (j + 1) * SHARE, :] = rolled[:, :CHUNK].astype(BF16)
        still = xt[:, pl.ds(start + PAD, CHUNK)]
        heads[0] += mm_nt(still, still)
        for shift in range(1, SCHUR_STEPS + 1):
            heads[shift] += mm_nt(moved[shift - 1], still)
        local[...] += mm_nt(still, columns[...])
        return carry

    lax.fori_loop(0, TIME // CHUNK, chunk_step, 0)
    scale = 1.0 / TIME
    heads[...] = heads[...] * scale
    for j in range(LOCAL):
        keep = jnp.where(lag0 + j >= 0, scale, 0.0)
        part = slice(j * SHARE, (j + 1) * SHARE)
        local[:, part] = local[:, part] * keep


def rows_product(out, left, right, finish):
    def step(i, carry):
        rows = pl.ds(pl.multiple_of(i * 128, 128), 128)
        value = jnp.dot(
            left[rows, :], right[...], precision=HIGHEST, preferred_element_type=F32
        )
        out[rows, :] = finish(value, rows)
        return carry

    lax.fori_loop(0, C // 128, step, 0)


def careful_solve(upper, lower, coeff, inverse, work, spare):
    head = upper[...]
    size = jnp.abs(head)
    bound = jnp.max(jnp.sum(size, axis=0)) * jnp.max(jnp.sum(size, axis=1))
    inverse[...] = head.T / bound

    def error(value, rows):
        place = rows.start + lax.broadcasted_iota(jnp.int32, (128, C), 0)
        cols = lax.broadcasted_iota(jnp.int32, (128, C), 1)
        return jnp.where(place == cols, 1.0, 0.0) - value

    def more(state):
        count, norm = state
        return jnp.logical_and(count < 100, norm > 1e-5)

    def newton(state):
        count, _ = state
        rows_product(work, upper, inverse, error)
        rows_product(spare, inverse, work, lambda v, rows: v + inverse[rows, :])
        inverse[...] = spare[...]
        return count + 1, jnp.sum(work[...] * work[...])

    lax.while_loop(more, newton, (0, jnp.float32(1e30)))
    rows_product(coeff, lower, inverse, lambda v, rows: v)
    rows_product(work, coeff, upper, lambda v, rows: lower[rows, :] - v)
    rows_product(spare, work, inverse, lambda v, rows: v + coeff[rows, :])
    coeff[...] = spare[...]


def solve(upper, lower, near, coeff, inverse, work, spare):
    low = lower[...]
    guess = mm(low.astype(BF16), near).astype(BF16)
    high, rest = halves(upper[...])
    left = low - mm(guess, high) - mm(guess, rest)
    error, size = jnp.sum(left * left), jnp.sum(low * low)
    coeff[...] = guess.astype(F32) + mm(left.astype(BF16), near)

    @pl.when(jnp.logical_not(error <= ACCEPT * size))
    def _():
        careful_solve(upper, lower, coeff, inverse, work, spare)


def kernel(place, *refs):
    sources = (refs[:5], refs[5:10])
    (out_upper, out_lower, xt, moved, columns, heads, local,
     up, low, near, coeff, inverse, work, spare, sem) = refs[10:]
    copies = load_blocks(place, sources, xt, sem)
    for copy in copies:
        copy.start()
    xt[:, :PAD] = jnp.zeros((C, PAD), BF16)
    xt[:, PAD + TIME :] = jnp.zeros((C, PAD), BF16)
    for copy in copies:
        copy.wait()
    products(place, xt, moved, columns, heads, local)

    one = eye()
    head = heads[0]
    weight = jnp.sum(head * one) / jnp.sum(head * head)
    err = (one - weight * head)
    err_b = err.astype(BF16)
    inv = weight * (one + err)
    err2 = mm(err_b, err_b).astype(BF16)
    inv = inv + mm(inv.astype(BF16), err2)
    err4 = mm(err2, err2).astype(BF16)
    inv = inv + mm(inv.astype(BF16), err4)
    near[...] = inv.astype(BF16)
    solve(heads.at[0], heads.at[1], near[...], coeff, inverse, work, spare)

    lag0 = LAG_DEV * place[1] - SCHUR_STEPS
    k = coeff[...]
    straight, turned = halves(k), halves(k.T)
    r1, r2 = halves(heads[1]), halves(heads[2])
    up[0] = heads[0] - mm3(turned, r1)
    up[1] = heads[1] - mm3(turned, r2)
    low[0] = heads[2] - mm3(straight, r1)
    low[1] = heads[3] - mm3(straight, r2)
    uppers = local[...]
    column = lax.broadcasted_iota(jnp.int32, (C, LOCAL * SHARE), 1)
    zero_lag = column // SHARE == -lag0
    lowers = jnp.where(zero_lag, 0.0, uppers)
    u = uppers[:, : 3 * SHARE] - mm3(turned, halves(lowers[:, SHARE : 4 * SHARE]))
    l = lowers[:, 2 * SHARE :] - mm3(straight, halves(uppers[:, SHARE : 4 * SHARE]))

    def closer(upper):
        before = near[...]
        err = one - mm(upper.astype(BF16), before)
        err_b = err.astype(BF16)
        inv = before.astype(F32) + mm(before, err_b)
        err2 = mm(err_b, err_b).astype(BF16)
        inv = inv + mm(inv.astype(BF16), err2)
        near[...] = inv.astype(BF16)

    closer(up[0])
    solve(up.at[0], low.at[0], near[...], coeff, inverse, work, spare)
    k = coeff[...]
    straight, turned = halves(k), halves(k.T)
    low[1] = low[1] - mm3(straight, halves(up[1]))
    up[0] = up[0] - mm3(turned, halves(low[0]))
    u, l = (
        u[:, : 2 * SHARE] - mm3(turned, halves(l[:, : 2 * SHARE])),
        l[:, SHARE:] - mm3(straight, halves(u[:, SHARE:])),
    )

    closer(up[0])
    solve(up.at[0], low.at[1], near[...], coeff, inverse, work, spare)
    k = coeff[...]
    straight, turned = halves(k), halves(k.T)
    u, l = u - mm3(turned, halves(l)), l - mm3(straight, halves(u))
    for i in range(LAG_DEV):
        out_upper[i] = u[:, i * SHARE : (i + 1) * SHARE]
        out_lower[i] = l[:, i * SHARE : (i + 1) * SHARE]


def eliminate(place, pieces):
    square = pltpu.VMEM((C, C), F32)
    out = jax.ShapeDtypeStruct((LAG_DEV, C, SHARE), F32)
    return pl.pallas_call(
        kernel,
        out_shape=(out, out),
        in_specs=[
            pl.BlockSpec(memory_space=pltpu.SMEM),
            *([pl.BlockSpec(memory_space=pl.ANY)] * len(pieces)),
        ],
        out_specs=(pl.BlockSpec(memory_space=pltpu.VMEM),) * 2,
        scratch_shapes=[
            pltpu.VMEM((C, PAD + TIME + PAD), BF16),
            pltpu.VMEM((SCHUR_STEPS, C, CHUNK), BF16),
            pltpu.VMEM((LOCAL * SHARE, CHUNK), BF16),
            pltpu.VMEM((4, C, C), F32),
            pltpu.VMEM((C, LOCAL * SHARE), F32),
            pltpu.VMEM((2, C, C), F32),
            pltpu.VMEM((2, C, C), F32),
            pltpu.VMEM((C, C), BF16),
            square,
            square,
            square,
            square,
            pltpu.SemaphoreType.DMA((TIME // HALF,)),
        ],
        compiler_params=pltpu.CompilerParams(vmem_limit_bytes=60 << 20),
        name="eliminate",
    )(place, *pieces)


AXES = ("y", "x", "z", "c")


def routes(sizes, move):
    y, x, z, c = sizes
    number = lambda p: ((p[0] % y * x + p[1] % x) * z + p[2] % z) * c + p[3] % c
    places = [
        (i, j, k, l) for i in range(y) for j in range(x) for k in range(z) for l in range(c)
    ]
    return [(number(p), number(move(*p))) for p in places]


def shards(sizes, samples):
    def along(axis, step):
        return routes(
            sizes,
            lambda y, x, z, c: (y, x + step, z, c) if c == axis else (y + step, x, z, c),
        )

    other = routes(sizes, lambda y, x, z, c: (y, x, z, 1 - c))
    send = lambda value, route: lax.ppermute(value, AXES, route)
    core = lax.axis_index("c")
    many = sizes[2] * sizes[3]
    block = lax.all_to_all(
        jnp.broadcast_to(samples[None], (many, *samples.shape)), ("z", "c"), 0, 0
    )
    block = block.reshape(BLOCK, C).T
    own = lax.dynamic_slice_in_dim(block, core * HALF, HALF, 1)

    before, after = send(own, along(0, 1)), send(own, along(0, -1))
    top, bottom = send(before[:HALF], along(0, 1)), send(after[HALF:], along(0, -1))
    across = jnp.concatenate([top, bottom], axis=0)
    own = jnp.stack([own, before, after, across])

    before, after = send(own, along(1, 1)), send(own, along(1, -1))
    own_other = send(own, other)
    top, bottom = send(before[:2], along(1, 1)), send(after[2:], along(1, -1))
    before_other, after_other = send(before, other), send(after, other)
    mine = (own, before, after, top, bottom)
    others = (own_other, before_other, after_other, send(top, other), send(bottom, other))
    place = jnp.stack(
        [
            lax.axis_index("y"),
            lax.axis_index(("x", "z", "c")),
            lax.axis_index("x"),
            core,
        ]
    ).astype(jnp.int32)
    return eliminate(place, mine + others)


def solution(mesh):
    sizes = (4, 4, 8, 2)
    fine = Mesh(mesh.devices.reshape(sizes), AXES)
    return jax.shard_map(
        functools.partial(shards, sizes),
        mesh=fine,
        in_specs=(P(AXES, None),),
        out_specs=(P(("x", "z", "c"), None, "y"),) * 2,
        check_vma=False,
    )
```

time: 1280 us -> 514 us (0.40)
  waiting for transfers between devices: 721 us -> 47.2 us
  Pallas kernels: 0 us -> 438 us
  other arithmetic: 384 us -> 0.75 us
  matrix products: 89.1 us -> 0 us
  local copies, waits for them, and re-layouts: 49.2 us -> 1.85 us
  between operations: 22.7 us -> 1.21 us
    psum x4 -> x0, waiting for transfers between devices: 634 us -> none  [the longest x3 573 us: spread(): return lax.psum(kept, axis)]
    pallas_call x0 -> x1, Pallas kernels: none -> 438 us  [eliminate(): pl.pallas_call(kernel, out_shape=(out, out), in_specs=[pl.BlockSpec(memor...]
    another operation x53 -> x3, other arithmetic: 368 us -> 0.75 us  [the longest x1 0.6 us: shards(): jnp.stack([lax.axis_index('y'), lax.axis_index(('x', 'z', 'c')), lax.axis...]
    all_gather x1 -> x0, waiting for transfers between devices: 83.1 us -> none  [shards(): window = lax.all_gather(samples, 'lag', axis=0, tiled=True)]
    dot_general x14 -> x0, matrix products: 45.3 us -> none  [the longest x3 13.8 us: shards(): lower = lower - jnp.einsum('ab,kbc->kac', coeff, upper, precision=HIGH)]
    another operation x60 -> x0, matrix products: 43.8 us -> none  [the longest x18 18 us: solve_coefficient(): factor = jnp.linalg.cholesky(normal)]
    another operation x52 -> x1, local copies, waits for them, and re-layouts: 34.2 us -> 0.02 us  [the longest x40 33.7 us: solve_coefficient(): lax.linalg.triangular_solve(factor, middle, left_side=True, lower=True, t...]
    ppermute x4 -> x13, waiting for transfers between devices: 3.34 us -> 31.3 us  [shards(): send = lambda value, route: lax.ppermute(value, AXES, route)]
  transfers between devices with their start and end apart: 9 -> 14, of which waited for: 6 -> 8; matrix products, arithmetic and copies ran while one was open for 26% -> 0% of each run, Pallas kernels for 0% -> 0%
where the time goes in v1:
time: 514 us; the launch traced here: 509 us
  Pallas kernels  438 us (85%)
  waiting for transfers between devices  47.2 us (9%)
  starting transfers between devices  19.9 us (4%)
    pallas_call x1, Pallas kernels, eliminate(): pl.pallas_call(kernel, out_shape=(out, out), in_specs=[pl.BlockSpec(memor...  438 us
    ppermute x13, waiting for transfers between devices, shards(): send = lambda value, route: lax.ppermute(value, AXES, route)  31.3 us
    all_to_all x1, waiting for transfers between devices, shards(): lax.all_to_all(jnp.broadcast_to(samples[None], (many, *samples.shape)), (...  15.9 us
    ppermute x13, starting transfers between devices, shards(): send = lambda value, route: lax.ppermute(value, AXES, route)  11.3 us
  transfers between devices with their start and end apart: 14, of which 8 were waited for; matrix products, arithmetic and copies ran while one was open for 0% of the time, Pallas kernels for 0%

profile of v1, /device:TPU:8, one launch (start us, length us, event | category | flops | bytes accessed | tf_op | source)
XLA Modules:
  0.0 508.9 jit_solution(7992700565252942800)
XLA Ops:
  0.6 1.6 broadcast_in_dim.2
  2.2 8.6 %all-to-all-start = ((bf16[16,32,512]{2,1,0:T(8,128)(2,1)}), bf16[16,32,512]{2,1,0:T(8,128)(2,1)S(1)}, u32[]{:S(2)}, u32[]{:S(2)}) async-start(bf16[16,32,512]{2,1,0:T(8,128)(2,1)} %broadcast_in_dim.2), calls=%async_computation | async-start | bytes 1048576 | tf_op jit(solution)/shard_map/all_to_all | solution.py:286
  10.8 15.9 %all-to-all-done = bf16[16,32,512]{2,1,0:T(8,128)(2,1)S(1)} async-done(((bf16[16,32,512]{2,1,0:T(8,128)(2,1)}), bf16[16,32,512]{2,1,0:T(8,128)(2,1)S(1)}, u32[]{:S(2)}, u32[]{:S(2)}) %all-to-all-start) | async-done | bytes 524320 | tf_op jit(solution)/shard_map/all_to_all | solution.py:286
  26.8 0.1 copy.5
  26.9 1.6 collective-permute-start
  28.5 1.7 collective-permute-start.1
  30.2 4.3 collective-permute-done
  34.6 0.4 collective-permute-start.2
  34.9 0.0 collective-permute-done.1
  35.0 3.0 collective-permute-start.3
  38.0 2.8 collective-permute-done.2
  40.8 0.0 collective-permute-done.3
  40.9 0.1 pad_maximum_fusion.refs_0_
  41.0 0.0 copy-start
  41.0 0.5 collective-permute-start.5
  41.5 1.6 collective-permute-start.4
  43.1 0.0 collective-permute-start.8
  43.1 12.8 %collective-permute-done.5.refs_2_ = bf16[4,512,256]{2,1,0:T(8,128)(2,1)S(1)} collective-permute-done((bf16[4,512,256]{2,1,0:T(8,128)(2,1)S(1)}, bf16[4,512,256]{2,1,0:T(8,128)(2,1)S(1)}, u32[]{:S(2)}, u32[]{:S(2)}) %collective-permute-start.5) | collective-permute-done | bytes 1048608 | tf_op jit(solution)/shard_map/ppermute | solution.py:283
  55.9 0.0 copy-start.1
  55.9 1.1 collective-permute-start.7
  57.0 0.3 collective-permute-done.4.refs_1_
  57.3 0.0 copy-start.2
  57.4 0.8 collective-permute-start.6
  58.2 0.0 collective-permute-start.10
  58.2 0.5 collective-permute-start.9
  58.7 6.6 %collective-permute-done.7.refs_4_ = bf16[2,512,256]{2,1,0:T(8,128)(2,1)} collective-permute-done((bf16[2,512,256]{2,1,0:T(8,128)(2,1)S(1)}, bf16[2,512,256]{2,1,0:T(8,128)(2,1)}, u32[]{:S(2)}, u32[]{:S(2)}) %collective-permute-start.7) | collective-permute-done | bytes 524320 | tf_op jit(solution)/shard_map/ppermute | solution.py:283
  65.3 0.0 collective-permute-start.12
  65.3 2.8 collective-permute-done.6.refs_3_
  68.1 0.2 collective-permute-start.11
  68.2 0.0 copy-done
  68.3 0.0 copy-done.1
  68.3 0.6 pad_add_fusion.place
  68.9 0.0 collective-permute-done.8.refs_5_
  68.9 0.0 collective-permute-done.12.refs_9_
  68.9 0.0 collective-permute-done.10.refs_7_
  68.9 1.6 collective-permute-done.11.refs_8_
  70.5 0.0 collective-permute-done.9.refs_6_
  70.5 0.0 copy-done.2
  70.5 438.0 %eliminate.1 = (f32[2,512,128]{2,1,0:T(8,128)}, f32[2,512,128]{2,1,0:T(8,128)}) custom-call(s32[4]{0:T(128)} %pad_add_fusion.place, bf16[4,512,256]{2,1,0:T(8,128)(2,1)} %copy-done, bf16[4,512,256]{2,1,0:T(8,128)(2,1)} %copy-done.2, bf16[4,512,256]{2,1,0:T(8,128)(2,1)} %copy-done.1, bf16[2,512,256]{2,1,0:T(8,128)(2,1)} %collective-permute-done.6.refs_3_, ...), custom_call_target="tpu_custom_call" | custom-call | tf_op jit(solution)/shard_map/eliminate/pallas_call | solution.py:235
  (6 shorter events, 0.1 us)
Async XLA Ops:
  2.2 24.5 %all-to-all-start = ((bf16[16,32,512]{2,1,0:T(8,128)(2,1)}), bf16[16,32,512]{2,1,0:T(8,128)(2,1)S(1)}, u32[]{:S(2)}, u32[]{:S(2)}) async-start(bf16[16,32,512]{2,1,0:T(8,128)(2,1)} %broadcast_in_dim.2), calls=%async_computation | async-start | bytes 1048576 | tf_op jit(solution)/shard_map/all_to_all | solution.py:286
  26.9 7.7 %collective-permute-start = (bf16[512,256]{1,0:T(8,128)(2,1)S(1)}, bf16[512,256]{1,0:T(8,128)(2,1)S(1)}, u32[]{:S(2)}, u32[]{:S(2)}) collective-permute-start(bf16[512,256]{1,0:T(8,128)(2,1)S(1)} %bitcast.13), channel_id=1, source_target_pairs={{0,16},{1,65},{2,18},{3,67},{4,20},{5,69},{6,22},{7,71},{8,24},{9,... | collective-permute-start | bytes 786440 | tf_op jit(solution)/shard_map/ppermute | solution.py:283
  28.5 6.5 %collective-permute-start.1 = (bf16[512,256]{1,0:T(8,128)(2,1)S(1)}, bf16[512,256]{1,0:T(8,128)(2,1)S(1)}, u32[]{:S(2)}, u32[]{:S(2)}) collective-permute-start(bf16[512,256]{1,0:T(8,128)(2,1)S(1)} %bitcast.14), channel_id=1, source_target_pairs={{0,48},{1,193},{2,50},{3,195},{4,52},{5,197},{6,54},{7,199},{8,56}... | collective-permute-start | bytes 786440 | tf_op jit(solution)/shard_map/ppermute | solution.py:283
  34.6 6.3 %collective-permute-start.2 = (bf16[256,256]{1,0:T(8,128)(2,1)S(1)}, bf16[256,256]{1,0:T(8,128)(2,1)S(1)}, u32[]{:S(2)}, u32[]{:S(2)}) collective-permute-start(bf16[256,256]{1,0:T(8,128)(2,1)S(1)} %slice.16), channel_id=1, source_target_pairs={{0,16},{1,65},{2,18},{3,67},{4,20},{5,69},{6,22},{7,71},{8,24},{9,... | collective-permute-start | bytes 393224 | tf_op jit(solution)/shard_map/ppermute | solution.py:283
  35.0 5.9 %collective-permute-start.3 = (bf16[256,256]{1,0:T(8,128)(2,1)S(1)}, bf16[256,256]{1,0:T(8,128)(2,1)S(1)}, u32[]{:S(2)}, u32[]{:S(2)}) collective-permute-start(bf16[256,256]{1,0:T(8,128)(2,1)S(1)} %slice.17), channel_id=1, source_target_pairs={{0,48},{1,193},{2,50},{3,195},{4,52},{5,197},{6,54},{7,199},{8,56}... | collective-permute-start | bytes 393224 | tf_op jit(solution)/shard_map/ppermute | solution.py:283
  41.0 27.2 %copy-start = (bf16[4,512,256]{2,1,0:T(8,128)(2,1)}, bf16[4,512,256]{2,1,0:T(8,128)(2,1)S(1)}, u32[]{:S(2)}) copy-start(bf16[4,512,256]{2,1,0:T(8,128)(2,1)S(1)} %pad_maximum_fusion.refs_0_) | copy-start | bytes 3145732
  41.0 14.9 %collective-permute-start.5 = (bf16[4,512,256]{2,1,0:T(8,128)(2,1)S(1)}, bf16[4,512,256]{2,1,0:T(8,128)(2,1)S(1)}, u32[]{:S(2)}, u32[]{:S(2)}) collective-permute-start(bf16[4,512,256]{2,1,0:T(8,128)(2,1)S(1)} %pad_maximum_fusion.refs_0_), channel_id=1, source_target_pairs={{0,192},{1,49},{2,194},{3,51},{4,196},{5,53},{6,198},{7,55},{8,200... | collective-permute-start | bytes 3145736 | tf_op jit(solution)/shard_map/ppermute | solution.py:283
  41.5 15.8 %collective-permute-start.4 = (bf16[4,512,256]{2,1,0:T(8,128)(2,1)S(1)}, bf16[4,512,256]{2,1,0:T(8,128)(2,1)S(1)}, u32[]{:S(2)}, u32[]{:S(2)}) collective-permute-start(bf16[4,512,256]{2,1,0:T(8,128)(2,1)S(1)} %pad_maximum_fusion.refs_0_), channel_id=1, source_target_pairs={{0,64},{1,17},{2,66},{3,19},{4,68},{5,21},{6,70},{7,23},{8,72},{9,... | collective-permute-start | bytes 3145736 | tf_op jit(solution)/shard_map/ppermute | solution.py:283
  43.1 25.8 %collective-permute-start.8 = (bf16[4,512,256]{2,1,0:T(8,128)(2,1)S(1)}, bf16[4,512,256]{2,1,0:T(8,128)(2,1)}, u32[]{:S(2)}, u32[]{:S(2)}) collective-permute-start(bf16[4,512,256]{2,1,0:T(8,128)(2,1)S(1)} %pad_maximum_fusion.refs_0_), channel_id=1, source_target_pairs={{0,1},{1,0},{2,3},{3,2},{4,5},{5,4},{6,7},{7,6},{8,9},{9,8},{10,11... | collective-permute-start | bytes 3145736 | tf_op jit(solution)/shard_map/ppermute | solution.py:283
  55.9 12.4 %copy-start.1 = (bf16[4,512,256]{2,1,0:T(8,128)(2,1)}, bf16[4,512,256]{2,1,0:T(8,128)(2,1)S(1)}, u32[]{:S(2)}) copy-start(bf16[4,512,256]{2,1,0:T(8,128)(2,1)S(1)} %collective-permute-done.5.refs_2_) | copy-start | bytes 3145732
  55.9 9.4 %collective-permute-start.7 = (bf16[2,512,256]{2,1,0:T(8,128)(2,1)S(1)}, bf16[2,512,256]{2,1,0:T(8,128)(2,1)}, u32[]{:S(2)}, u32[]{:S(2)}) collective-permute-start(bf16[2,512,256]{2,1,0:T(8,128)(2,1)S(1)} %slice.19), channel_id=1, source_target_pairs={{0,192},{1,49},{2,194},{3,51},{4,196},{5,53},{6,198},{7,55},{8,200... | collective-permute-start | bytes 1572872 | tf_op jit(solution)/shard_map/ppermute | solution.py:283
  57.3 13.2 %copy-start.2 = (bf16[4,512,256]{2,1,0:T(8,128)(2,1)}, bf16[4,512,256]{2,1,0:T(8,128)(2,1)S(1)}, u32[]{:S(2)}) copy-start(bf16[4,512,256]{2,1,0:T(8,128)(2,1)S(1)} %collective-permute-done.4.refs_1_) | copy-start | bytes 3145732
  57.4 10.7 %collective-permute-start.6 = (bf16[2,512,256]{2,1,0:T(8,128)(2,1)S(1)}, bf16[2,512,256]{2,1,0:T(8,128)(2,1)}, u32[]{:S(2)}, u32[]{:S(2)}) collective-permute-start(bf16[2,512,256]{2,1,0:T(8,128)(2,1)S(1)} %slice.18), channel_id=1, source_target_pairs={{0,64},{1,17},{2,66},{3,19},{4,68},{5,21},{6,70},{7,23},{8,72},{9,... | collective-permute-start | bytes 1572872 | tf_op jit(solution)/shard_map/ppermute | solution.py:283
  58.2 10.7 %collective-permute-start.10 = (bf16[4,512,256]{2,1,0:T(8,128)(2,1)S(1)}, bf16[4,512,256]{2,1,0:T(8,128)(2,1)}, u32[]{:S(2)}, u32[]{:S(2)}) collective-permute-start(bf16[4,512,256]{2,1,0:T(8,128)(2,1)S(1)} %collective-permute-done.5.refs_2_), channel_id=1, source_target_pairs={{0,1},{1,0},{2,3},{3,2},{4,5},{5,4},{6,7},{7,6},{8,9},{9,8},{10,11... | collective-permute-start | bytes 3145736 | tf_op jit(solution)/shard_map/ppermute | solution.py:283
  58.2 12.3 %collective-permute-start.9 = (bf16[4,512,256]{2,1,0:T(8,128)(2,1)S(1)}, bf16[4,512,256]{2,1,0:T(8,128)(2,1)}, u32[]{:S(2)}, u32[]{:S(2)}) collective-permute-start(bf16[4,512,256]{2,1,0:T(8,128)(2,1)S(1)} %collective-permute-done.4.refs_1_), channel_id=1, source_target_pairs={{0,1},{1,0},{2,3},{3,2},{4,5},{5,4},{6,7},{7,6},{8,9},{9,8},{10,11... | collective-permute-start | bytes 3145736 | tf_op jit(solution)/shard_map/ppermute | solution.py:283
  65.3 3.6 collective-permute-start.12
  68.1 2.4 collective-permute-start.11
